TPU v7x, 512 devices: a whole 4x8x8 slice. The times are simulated.
512 devices in a mesh: shard: 64 (over x, z, core), rep: 8 (over y).
Axes of the slice: x: 4, y: 8, z: 8, core: 2. Of those that a mesh axis runs over, the one named last changes fastest.
Arguments:
- attn_grad: bfloat16 [8, 2, 4, 768, 768], P('rep', None, None, 'shard'), may hold values from -16 to 16
- attn_error: float32 [8, 2, 4, 768, 768], P('rep', None, None, 'shard'), may hold values from -6 to 6
- attn_basis: float32 [2, 4, 768, 32], P(None, None, 'shard'), may hold values from -0.21875 to 0.21875
- attn_roots: float32 [2, 4, 3, 32, 32], replicated, as said below
- attn_momentum: float32 [2, 4, 768, 768], P(None, None, 'shard'), may hold values from -4 to 4
- attn_weights: float32 [2, 4, 768, 768], P(None, None, 'shard'), may hold values from -0.21875 to 0.21875
- mlp_grad: bfloat16 [8, 2, 2, 768, 3072], P('rep', None, None, 'shard'), may hold values from -16 to 16
- mlp_error: float32 [8, 2, 2, 768, 3072], P('rep', None, None, 'shard'), may hold values from -6 to 6
- mlp_basis: float32 [2, 2, 3072, 32], P(None, None, 'shard'), may hold values from -0.109375 to 0.109375
- mlp_roots: float32 [2, 2, 3, 32, 32], replicated, as said below
- mlp_momentum: float32 [2, 2, 768, 3072], P(None, None, 'shard'), may hold values from -4 to 4
- mlp_weights: float32 [2, 2, 768, 3072], P(None, None, 'shard'), may hold values from -0.21875 to 0.21875
- small_grad: bfloat16 [8, 2, 9984], P('rep', None, 'shard'), may hold values from -6 to 6
- small_momentum: float32 [2, 9984], P(None, 'shard'), may hold values from -4 to 4
- small_weights: float32 [2, 9984], P(None, 'shard'), may hold values from -6 to 6
Outputs:
- attn_error_out: float32 [8, 2, 4, 768, 768], P('rep', None, None, 'shard')
- mlp_error_out: float32 [8, 2, 2, 768, 3072], P('rep', None, None, 'shard')
- attn_left: float32 [2, 4, 768, 32], P(None, None, 'shard')
- attn_right: float32 [2, 4, 768, 32], P(None, None, 'shard')
- mlp_left: float32 [2, 2, 768, 32], P(None, None, 'shard')
- mlp_right: float32 [2, 2, 3072, 32], P(None, None, 'shard')
- attn_momentum_out: float32 [2, 4, 768, 768], P(None, None, 'shard')
- attn_weights_out: float32 [2, 4, 768, 768], P(None, None, 'shard')
- mlp_momentum_out: float32 [2, 2, 768, 3072], P(None, None, 'shard')
- mlp_weights_out: float32 [2, 2, 768, 3072], P(None, None, 'shard')
- small_momentum_out: float32 [2, 9984], P(None, 'shard')
- small_weights_out: float32 [2, 9984], P(None, 'shard')
Inputs may be any that keep to these rules, and one draw needn't show every extreme that they name: Every 32 x 32 factor of attn_roots is a scaled identity plus independent entries and is well conditioned. Every 32 x 32 factor of mlp_roots is a scaled identity plus independent entries and is well conditioned.
All inputs are finite; a program needn't handle non-finite values.
Results may differ from a plain program's by a relative error of at most 0.0003.
Values sent between devices are 32-bit elements; how exact they have to be, the bound alone decides.
A program may use at most 64 MiB of HBM per device.

v0:
```python
import jax
import jax.numpy as jnp
from jax import lax
from jax.sharding import PartitionSpec as P

momentum_decay = 0.9
learn_rate = 0.05


def rows_product(merged, factor):
    return jnp.einsum("lkrc,lkcn->lkrn", merged, factor, precision=lax.Precision.HIGHEST)


def cols_product(merged, factor):
    return jnp.einsum("lkrc,lkrn->lkcn", merged, factor, precision=lax.Precision.HIGHEST)


def rotate(factor, inverse_roots, round_index):
    return jnp.einsum(
        "lkrn,lknm->lkrm", factor, inverse_roots[:, :, round_index], precision=lax.Precision.HIGHEST
    )


def finish(summed, inverse_roots, round_index):
    if round_index < 0:
        return summed / float(lax.axis_size("rep"))
    return rotate(summed, inverse_roots, round_index)


def own_share(full_factor):
    share_width = full_factor.shape[2] // lax.axis_size("shard")
    share_start = lax.axis_index("shard") * share_width
    return lax.dynamic_slice_in_dim(full_factor, share_start, share_width, 2)


def column_round(attn_term, mlp_term, attn_roots, mlp_roots, round_index):
    attn_full, mlp_full = lax.psum((attn_term, mlp_term), ("shard", "rep"))
    attn_full = finish(attn_full, attn_roots, round_index)
    mlp_full = finish(mlp_full, mlp_roots, round_index)
    attn_share = own_share(attn_full)
    mlp_share = own_share(mlp_full)
    attn_next, mlp_next = (attn_full, mlp_full)
    return (attn_next, mlp_next, attn_full, mlp_full, attn_share, mlp_share)


def update(merged, approx, momentum, weights):
    error_out = (merged - approx)[None]
    momentum_out = momentum_decay * momentum + approx
    weights_out = weights - learn_rate * momentum_out
    return (error_out, momentum_out, weights_out)


def per_device(
    attn_grad,
    attn_error,
    attn_basis,
    attn_roots,
    attn_momentum,
    attn_weights,
    mlp_grad,
    mlp_error,
    mlp_basis,
    mlp_roots,
    mlp_momentum,
    mlp_weights,
    small_grad,
    small_momentum,
    small_weights,
):
    attn_merged = attn_grad[0].astype(jnp.float32) + attn_error[0]
    mlp_merged = mlp_grad[0].astype(jnp.float32) + mlp_error[0]
    small_local = small_grad[0].astype(jnp.float32)
    attn_bfull, mlp_bfull = (
        lax.all_gather(attn_basis, "shard", axis=2, tiled=True),
        lax.all_gather(mlp_basis, "shard", axis=2, tiled=True),
    )
    attn_data, mlp_data = (attn_merged, mlp_merged)
    attn_start, mlp_start = (attn_bfull, mlp_bfull)
    attn_first = rows_product(attn_data, attn_start)
    mlp_first = rows_product(mlp_data, mlp_start)
    small_total = lax.psum(small_local, "rep")
    attn_first, mlp_first = lax.psum((attn_first, mlp_first), "rep")
    attn_lhat = rotate(attn_first, attn_roots, 0)
    mlp_lhat = rotate(mlp_first, mlp_roots, 0)
    attn_rhat, mlp_rhat, spare_one, spare_two, spare_three, spare_four = column_round(
        cols_product(attn_data, attn_lhat),
        cols_product(mlp_data, mlp_lhat),
        attn_roots,
        mlp_roots,
        1,
    )
    attn_second, mlp_second = lax.psum(
        (rows_product(attn_data, attn_rhat), rows_product(mlp_data, mlp_rhat)), "rep"
    )
    attn_left = rotate(attn_second, attn_roots, 2)
    mlp_left = rotate(mlp_second, mlp_roots, 2)
    spare_five, spare_six, attn_rfull, mlp_rfull, attn_right, mlp_right = column_round(
        cols_product(attn_data, attn_left),
        cols_product(mlp_data, mlp_left),
        attn_roots,
        mlp_roots,
        -1,
    )
    attn_approx = jnp.einsum(
        "lkrn,lkcn->lkrc", attn_left, attn_rfull, precision=lax.Precision.HIGHEST
    )
    mlp_approx = jnp.einsum("lkrn,lkcn->lkrc", mlp_left, mlp_rfull, precision=lax.Precision.HIGHEST)
    attn_error_out, attn_momentum_out, attn_weights_out = update(
        attn_merged, attn_approx, attn_momentum, attn_weights
    )
    mlp_error_out, mlp_momentum_out, mlp_weights_out = update(
        mlp_merged, mlp_approx, mlp_momentum, mlp_weights
    )
    small_mean = small_total / float(lax.axis_size("rep"))
    small_momentum_out = momentum_decay * small_momentum + small_mean
    small_weights_out = small_weights - learn_rate * small_momentum_out
    return (
        attn_error_out,
        mlp_error_out,
        attn_left,
        attn_right,
        mlp_left,
        mlp_right,
        attn_momentum_out,
        attn_weights_out,
        mlp_momentum_out,
        mlp_weights_out,
        small_momentum_out,
        small_weights_out,
    )


def solution(mesh):
    in_specs = (
        P("rep", None, None, "shard", None),
        P("rep", None, None, "shard", None),
        P(None, None, "shard", None),
        P(),
        P(None, None, "shard", None),
        P(None, None, "shard", None),
        P("rep", None, None, "shard", None),
        P("rep", None, None, "shard", None),
        P(None, None, "shard", None),
        P(),
        P(None, None, "shard", None),
        P(None, None, "shard", None),
        P("rep", None, "shard"),
        P(None, "shard"),
        P(None, "shard"),
    )
    out_specs = (
        P("rep", None, None, "shard", None),
        P("rep", None, None, "shard", None),
        P(None, None, "shard", None),
        P(None, None, "shard", None),
        P(None, None, "shard", None),
        P(None, None, "shard", None),
        P(None, None, "shard", None),
        P(None, None, "shard", None),
        P(None, None, "shard", None),
        P(None, None, "shard", None),
        P(None, "shard"),
        P(None, "shard"),
    )
    return jax.shard_map(
        per_device, mesh=mesh, in_specs=in_specs, out_specs=out_specs, check_vma=False
    )
```

profile of v0, /device:TPU:1, one launch (start us, length us, event | category | flops | bytes accessed | tf_op | source)
XLA Modules:
  0.0 757.0 jit_solution(16800400785792100691)
XLA Ops:
  7.2 0.0 all-gather.2.cloned.1.call-start
  7.2 1.6 copy.101
  8.8 0.0 all-gather.2.cloned.1.call-update
  8.8 0.0 all-reduce.9.cloned.1.call-start
  8.9 0.8 copy.94
  9.7 0.0 copy-start.3
  9.7 59.7 %all_gather.6 = f32[2,4,768,32]{3,1,0,2:T(4,128)S(1)} all-gather(f32[2,4,12,32]{3,1,0,2:T(4,128)S(1)} %copy.94), channel_id=1, replica_groups=mesh['shard'=64,'rep'=8] {'shard'}, dimensions={2}, use_global_device_ids=true | all-gather | bytes 798720 | tf_op jit(solution)/shard_map/all_gather | solution.py:74
  69.4 2.1 fusion.2
  71.6 33.6 %all-gather.2.cloned.1.call-done = f32[2,2,3072,32]{3,1,0,2:T(2,128)} async-done(((f32[2,2,48,32]{3,1,0,2:T(2,128)}), f32[2,2,3072,32]{3,1,0,2:T(2,128)}) %all-gather.2.cloned.1.call-update) | async-done | bytes 1572880 | tf_op jit(solution)/shard_map/all_gather | solution.py:75
  105.2 6.1 fusion
  111.3 23.7 %all-reduce.3 = (f32[2,4,12,32]{3,2,1,0:T(8,128)S(1)}, f32[2,2,12,32]{3,2,1,0:T(8,128)S(1)}) all-reduce(f32[2,4,12,32]{3,2,1,0:T(8,128)S(1)} %fusion.2, f32[2,2,12,32]{3,2,1,0:T(8,128)S(1)} %fusion), channel_id=1, replica_groups=mesh['shard'=64,'rep'=8] {'rep'}, use_global_device_ids=true, to_apply=%region_0.0 | all-reduce | flops 4608 | bytes 36864 | tf_op jit(solution)/shard_map/psum | solution.py:82
  135.1 0.2 fusion.26
  135.3 1.7 fusion.17
  137.0 0.2 fusion.35
  137.2 2.8 fusion.8
  140.0 0.0 all-reduce.9.cloned.1.call-update
  140.0 0.2 all-reduce.7.cloned.1.call-start
  140.3 0.4 copy-done.15
  140.7 279.9 %all-reduce.9.cloned.1.call-done = (f32[2,4,768,32]{2,3,1,0:T(8,128)}, f32[2,2,3072,32]{2,3,1,0:T(8,128)}) async-done(((f32[2,4,768,32]{2,3,1,0:T(8,128)}, f32[2,2,3072,32]{2,3,1,0:T(8,128)}), (f32[2,4,768,32]{2,3,1,0:T(8,128)}, f32[2,2,3072,32]{2,3,1,0:T(8,128)})) %all-reduce.9.cloned.1.call-update) | async-done | bytes 2359312 | tf_op jit(solution)/shard_map/psum | solution.py:37
  420.6 2.1 fusion.22
  422.7 0.8 fusion.15
  423.5 1.5 fusion.31
  424.9 1.6 fusion.6
  426.6 23.4 %all-reduce.2 = (f32[2,4,12,32]{3,2,1,0:T(8,128)S(1)}, f32[2,2,12,32]{3,2,1,0:T(8,128)S(1)}, f32[2,156]{1,0:T(2,128)S(1)}) all-reduce(f32[2,4,12,32]{3,2,1,0:T(8,128)S(1)} %fusion.15, f32[2,2,12,32]{3,2,1,0:T(8,128)S(1)} %fusion.6, f32[2,156]{1,0:T(2,128)S(1)} %bitcast_convert_fusion), channel_id=1, replica_groups=mesh['shard'=64,'rep'=8] {'rep'}, use_global_device_ids=true, to_apply=%region_2.0 | all-reduce | flops 4920 | bytes 39360 | tf_op jit(solution)/shard_map/psum | solution.py:92
  450.0 0.2 fusion.24
  450.2 0.2 fusion.33
  450.4 1.7 fusion.13
  452.1 2.8 fusion.4
  454.9 0.0 all-reduce.7.cloned.1.call-update
  454.9 0.6 copy.114
  455.6 0.6 copy.112
  456.2 0.6 multiply_subtract_fusion
  456.8 280.8 %all-reduce.7.cloned.1.call-done = (f32[2,4,768,32]{2,3,1,0:T(8,128)}, f32[2,2,3072,32]{2,3,1,0:T(8,128)}) async-done(((f32[2,4,768,32]{2,3,1,0:T(8,128)}, f32[2,2,3072,32]{2,3,1,0:T(8,128)}), (f32[2,4,768,32]{2,3,1,0:T(8,128)}, f32[2,2,3072,32]{2,3,1,0:T(8,128)})) %all-reduce.7.cloned.1.call-update) | async-done | bytes 2359312 | tf_op jit(solution)/shard_map/psum | solution.py:37
  737.6 1.3 broadcast_multiply_fusion.1
  738.9 0.1 constant_dynamic-slice_fusion.1
  739.0 0.7 copy.113
  739.7 0.7 copy_subtract_fusion.1
  740.4 0.9 copy.116
  741.3 0.9 copy.115
  742.2 0.9 copy.110
  743.1 0.1 broadcast_multiply_fusion
  743.3 0.9 copy-done.7
  744.2 0.2 copy-done.8
  744.4 1.5 copy_subtract_fusion
  745.9 1.3 copy.118
  747.2 1.3 copy.117
  748.5 1.3 copy.111
  749.7 0.7 constant_dynamic-slice_fusion
  (29 shorter events, 0.1 us)
Async XLA Ops:
  7.2 98.0 %all-gather.2.cloned.1.call-start = ((), (), s32[]{:S(2)}) async-start(), calls=%async_computation | async-start | bytes 6389760 | tf_op jit(solution)/shard_map/all_gather | solution.py:75
  8.8 411.8 %all-reduce.9.cloned.1.call-start = ((), (), s32[]{:S(2)}) async-start(), calls=%async_computation.2 | async-start | bytes 4718592 | tf_op jit(solution)/shard_map/psum | solution.py:37
  9.7 59.7 %copy-start.2 = (f32[1,2,4,12,768]{4,2,3,1,0:T(4,128)S(1)}, f32[1,2,4,12,768]{4,2,3,1,0:T(4,128)}, u32[]{:S(2)}) copy-start(f32[1,2,4,12,768]{4,2,3,1,0:T(4,128)} %param.16) | copy-start | bytes 884740
  9.7 59.7 %copy-start.3 = (bf16[1,2,4,12,768]{4,2,3,1,0:T(4,128)(2,1)S(1)}, bf16[1,2,4,12,768]{4,2,3,1,0:T(4,128)(2,1)}, u32[]{:S(2)}) copy-start(bf16[1,2,4,12,768]{4,2,3,1,0:T(4,128)(2,1)} %param.15) | copy-start | bytes 442372
  69.4 35.8 %copy-start = (f32[1,2,2,12,3072]{4,2,3,1,0:T(2,128)S(1)}, f32[1,2,2,12,3072]{4,2,3,1,0:T(2,128)}, u32[]{:S(2)}) copy-start(f32[1,2,2,12,3072]{4,2,3,1,0:T(2,128)} %param.22) | copy-start | bytes 1769476
  69.4 35.8 %copy-start.1 = (bf16[1,2,2,12,3072]{4,2,3,1,0:T(2,128)(2,1)S(1)}, bf16[1,2,2,12,3072]{4,2,3,1,0:T(2,128)(2,1)}, u32[]{:S(2)}) copy-start(bf16[1,2,2,12,3072]{4,2,3,1,0:T(2,128)(2,1)} %param.21) | copy-start | bytes 884740
  71.5 63.5 %copy-start.11 = (f32[2,4,3,32,32]{4,3,2,1,0:T(8,128)S(1)}, f32[2,4,3,32,32]{4,3,2,1,0:T(8,128)}, u32[]{:S(2)}) copy-start(f32[2,4,3,32,32]{4,3,2,1,0:T(8,128)} %param.18) | copy-start | bytes 294916
  111.3 25.7 %copy-start.12 = (f32[2,2,3,32,32]{4,3,2,1,0:T(8,128)S(1)}, f32[2,2,3,32,32]{4,3,2,1,0:T(8,128)}, u32[]{:S(2)}) copy-start(f32[2,2,3,32,32]{4,3,2,1,0:T(8,128)} %param.24) | copy-start | bytes 147460
  140.0 0.7 copy-start.15
  140.0 597.6 %all-reduce.7.cloned.1.call-start = ((), (), s32[]{:S(2)}) async-start(), calls=%async_computation.1 | async-start | bytes 4718592 | tf_op jit(solution)/shard_map/psum | solution.py:37
  420.6 2.9 copy-start.6
  454.9 1.3 copy-start.13
  454.9 1.3 copy-start.14
  454.9 284.8 %copy-start.9 = (f32[2,4,12,768]{3,1,2,0:T(4,128)S(1)}, f32[2,4,12,768]{3,1,2,0:T(4,128)}, u32[]{:S(2)}) copy-start(f32[2,4,12,768]{3,1,2,0:T(4,128)} %param.20) | copy-start | bytes 884740
  454.9 284.8 %copy-start.10 = (f32[2,4,12,768]{3,1,2,0:T(4,128)S(1)}, f32[2,4,12,768]{3,1,2,0:T(4,128)}, u32[]{:S(2)}) copy-start(f32[2,4,12,768]{3,1,2,0:T(4,128)} %param.19) | copy-start | bytes 884740
  737.6 2.1 copy-start.5
  740.4 2.7 copy-start.4
  743.1 1.1 copy-start.7
  743.1 1.2 copy-start.8
Sparse Core Ops, SparseCore 0:
  11.9 93.1 all-gather.1
  140.1 280.3 all-reduce.8
  455.0 282.5 all-reduce.6
where the time goes:
time: 757 us
  waiting for transfers between devices  594 us (78%)
  blocking collectives  107 us (14%)
  matrix products  26.2 us (3%)
  between operations  14 us (2%)
  local copies, waits for them, and re-layouts  13.3 us (2%)
    psum x2, waiting for transfers between devices, column_round(): attn_full, mlp_full = lax.psum((attn_term, mlp_term), ('shard', 'rep'))  561 us
    all_gather x1, blocking collectives, per_device(): lax.all_gather(attn_basis, 'shard', axis=2, tiled=True)  59.7 us
    all_gather x1, waiting for transfers between devices, per_device(): lax.all_gather(mlp_basis, 'shard', axis=2, tiled=True)  33.6 us
    psum x1, blocking collectives, per_device(): attn_first, mlp_first = lax.psum((attn_first, mlp_first), 'rep')  23.7 us
    psum x1, blocking collectives, per_device(): lax.psum((rows_product(attn_data, attn_rhat), rows_product(mlp_data, mlp_...  23.4 us
  transfers between devices with their start and end apart: 3, of which 3 were waited for; matrix products, arithmetic and copies ran while one was open for 1% of the time, Pallas kernels for 0%

commit v1 on v0

--- a/solution.py
+++ b/solution.py
@@ -5,6 +5,11 @@
 
 momentum_decay = 0.9
 learn_rate = 0.05
+
+
+def one_after_other(array, one, other):
+    half = lax.psum(array, one)
+    return lax.psum(half, other)
 
 
 def rows_product(merged, factor):
@@ -34,7 +39,7 @@
 
 
 def column_round(attn_term, mlp_term, attn_roots, mlp_roots, round_index):
-    attn_full, mlp_full = lax.psum((attn_term, mlp_term), ("shard", "rep"))
+    attn_full, mlp_full = one_after_other((attn_term, mlp_term), "shard", "rep")
     attn_full = finish(attn_full, attn_roots, round_index)
     mlp_full = finish(mlp_full, mlp_roots, round_index)
     attn_share = own_share(attn_full)

time: 757 us -> 784 us (1.036)
  waiting for transfers between devices: 594 us -> 618 us
    psum x2 -> x4, waiting for transfers between devices: 561 us -> 585 us  [the longest x2 410 us: one_after_other(): half = lax.psum(array, one)]
  transfers between devices with their start and end apart: 3 -> 5, of which waited for: 3 -> 5; matrix products, arithmetic and copies ran while one was open for 1% -> 1% of each run, Pallas kernels for 0% -> 0%
where the time goes in v1:
time: 784 us; the launch traced here: 781 us
  waiting for transfers between devices  618 us (79%)
  blocking collectives  107 us (14%)
  matrix products  26.2 us (3%)
  between operations  14 us (2%)
  local copies, waits for them, and re-layouts  12.9 us (2%)
    psum x2, waiting for transfers between devices, one_after_other(): half = lax.psum(array, one)  410 us
    psum x2, waiting for transfers between devices, one_after_other(): return lax.psum(half, other)  174 us
    all_gather x1, blocking collectives, per_device(): lax.all_gather(attn_basis, 'shard', axis=2, tiled=True)  59.7 us
    all_gather x1, waiting for transfers between devices, per_device(): lax.all_gather(mlp_basis, 'shard', axis=2, tiled=True)  33.6 us
    psum x1, blocking collectives, per_device(): attn_first, mlp_first = lax.psum((attn_first, mlp_first), 'rep')  23.7 us
    psum x1, blocking collectives, per_device(): lax.psum((rows_product(attn_data, attn_rhat), rows_product(mlp_data, mlp_...  23.6 us
  transfers between devices with their start and end apart: 5, of which 5 were waited for; matrix products, arithmetic and copies ran while one was open for 1% of the time, Pallas kernels for 0%

profile of v1, /device:TPU:1, one launch (start us, length us, event | category | flops | bytes accessed | tf_op | source)
XLA Modules:
  0.0 781.0 jit_solution(3708317513811696136)
XLA Ops:
  7.2 0.0 all-gather.2.cloned.1.call-start
  7.2 1.6 copy.101
  8.8 0.0 all-reduce.13.cloned.1.call-start
  8.9 0.8 copy.94
  9.7 59.7 %all_gather.6 = f32[2,4,768,32]{3,1,0,2:T(4,128)S(1)} all-gather(f32[2,4,12,32]{3,1,0,2:T(4,128)S(1)} %copy.94), channel_id=1, replica_groups=mesh['shard'=64,'rep'=8] {'shard'}, dimensions={2}, use_global_device_ids=true | all-gather | bytes 798720 | tf_op jit(solution)/shard_map/all_gather | solution.py:79
  69.4 2.1 fusion.2
  71.6 33.6 %all-gather.2.cloned.1.call-done = f32[2,2,3072,32]{3,1,0,2:T(2,128)} async-done(((f32[2,2,48,32]{3,1,0,2:T(2,128)}), f32[2,2,3072,32]{3,1,0,2:T(2,128)}) %all-gather.2.cloned.1.call-update) | async-done | bytes 1572880 | tf_op jit(solution)/shard_map/all_gather | solution.py:80
  105.2 6.1 fusion
  111.3 23.7 %all-reduce.3 = (f32[2,4,12,32]{3,2,1,0:T(8,128)S(1)}, f32[2,2,12,32]{3,2,1,0:T(8,128)S(1)}) all-reduce(f32[2,4,12,32]{3,2,1,0:T(8,128)S(1)} %fusion.2, f32[2,2,12,32]{3,2,1,0:T(8,128)S(1)} %fusion), channel_id=1, replica_groups=mesh['shard'=64,'rep'=8] {'rep'}, use_global_device_ids=true, to_apply=%region_0.0 | all-reduce | flops 4608 | bytes 36864 | tf_op jit(solution)/shard_map/psum | solution.py:87
  135.1 0.2 fusion.26
  135.3 1.7 fusion.17
  137.0 0.2 fusion.35
  137.2 2.8 fusion.8
  140.0 0.0 all-reduce.13.cloned.1.call-update
  140.0 0.0 all-reduce.17.cloned.1.call-start
  140.1 201.0 %all-reduce.13.cloned.1.call-done = (f32[2,4,768,32]{2,3,1,0:T(8,128)}, f32[2,2,3072,32]{2,3,1,0:T(8,128)}) async-done(((f32[2,4,768,32]{2,3,1,0:T(8,128)}, f32[2,2,3072,32]{2,3,1,0:T(8,128)}), (f32[2,4,768,32]{2,3,1,0:T(8,128)}, f32[2,2,3072,32]{2,3,1,0:T(8,128)})) %all-reduce.13.cloned.1.call-update) | async-done | bytes 2359312 | tf_op jit(solution)/shard_map/psum | solution.py:11
  341.1 0.2 all-reduce.11.cloned.1.call-start
  341.3 88.0 %all-reduce.17.cloned.1.call-done = (f32[2,4,768,32]{2,3,1,0:T(8,128)}, f32[2,2,3072,32]{2,3,1,0:T(8,128)}) async-done(((f32[2,4,768,32]{2,3,1,0:T(8,128)}, f32[2,2,3072,32]{2,3,1,0:T(8,128)}), (f32[2,4,768,32]{2,3,1,0:T(8,128)}, f32[2,2,3072,32]{2,3,1,0:T(8,128)})) %all-reduce.17.cloned.1.call-update) | async-done | bytes 2359312 | tf_op jit(solution)/shard_map/psum | solution.py:12
  429.3 2.1 fusion.22
  431.4 0.8 fusion.15
  432.2 1.5 fusion.31
  433.7 1.6 fusion.6
  435.3 23.6 %all-reduce.2 = (f32[2,4,12,32]{3,2,1,0:T(8,128)S(1)}, f32[2,2,12,32]{3,2,1,0:T(8,128)S(1)}, f32[2,156]{1,0:T(2,128)S(1)}) all-reduce(f32[2,4,12,32]{3,2,1,0:T(8,128)S(1)} %fusion.15, f32[2,2,12,32]{3,2,1,0:T(8,128)S(1)} %fusion.6, f32[2,156]{1,0:T(2,128)S(1)} %bitcast_convert_fusion), channel_id=1, replica_groups=mesh['shard'=64,'rep'=8] {'rep'}, use_global_device_ids=true, to_apply=%region_3.0 | all-reduce | flops 4920 | bytes 39360 | tf_op jit(solution)/shard_map/psum | solution.py:97
  458.9 0.2 fusion.24
  459.2 0.2 fusion.33
  459.4 1.7 fusion.13
  461.1 2.8 fusion.4
  463.9 0.3 all-reduce.15.cloned.1.call-start
  464.2 209.3 %all-reduce.11.cloned.1.call-done = (f32[2,4,768,32]{2,3,1,0:T(8,128)}, f32[2,2,3072,32]{2,3,1,0:T(8,128)}) async-done(((f32[2,4,768,32]{2,3,1,0:T(8,128)}, f32[2,2,3072,32]{2,3,1,0:T(8,128)}), (f32[2,4,768,32]{2,3,1,0:T(8,128)}, f32[2,2,3072,32]{2,3,1,0:T(8,128)})) %all-reduce.11.cloned.1.call-update) | async-done | bytes 2359312 | tf_op jit(solution)/shard_map/psum | solution.py:11
  673.6 0.6 copy.114
  674.2 0.6 copy.112
  674.8 0.6 multiply_subtract_fusion
  675.4 86.2 %all-reduce.15.cloned.1.call-done = (f32[2,4,768,32]{2,3,1,0:T(8,128)}, f32[2,2,3072,32]{2,3,1,0:T(8,128)}) async-done(((f32[2,4,768,32]{2,3,1,0:T(8,128)}, f32[2,2,3072,32]{2,3,1,0:T(8,128)}), (f32[2,4,768,32]{2,3,1,0:T(8,128)}, f32[2,2,3072,32]{2,3,1,0:T(8,128)})) %all-reduce.15.cloned.1.call-update) | async-done | bytes 2359312 | tf_op jit(solution)/shard_map/psum | solution.py:12
  761.7 1.3 broadcast_multiply_fusion.1
  762.9 0.1 constant_dynamic-slice_fusion.1
  763.0 0.7 copy.113
  763.8 0.7 copy_subtract_fusion.1
  764.5 0.9 copy.116
  765.4 0.9 copy.115
  766.3 0.9 copy.110
  767.2 0.1 broadcast_multiply_fusion
  767.4 0.9 copy-done.7
  768.3 0.2 copy-done.8
  768.4 1.5 copy_subtract_fusion
  770.0 1.3 copy.118
  771.3 1.3 copy.117
  772.5 1.3 copy.111
  773.8 0.7 constant_dynamic-slice_fusion
  (35 shorter events, 0.2 us)
Async XLA Ops:
  7.2 98.0 %all-gather.2.cloned.1.call-start = ((), (), s32[]{:S(2)}) async-start(), calls=%async_computation | async-start | bytes 6389760 | tf_op jit(solution)/shard_map/all_gather | solution.py:80
  8.8 332.2 %all-reduce.13.cloned.1.call-start = ((), (), s32[]{:S(2)}) async-start(), calls=%async_computation.2 | async-start | bytes 4718592 | tf_op jit(solution)/shard_map/psum | solution.py:11
  9.7 59.7 %copy-start.2 = (f32[1,2,4,12,768]{4,2,3,1,0:T(4,128)S(1)}, f32[1,2,4,12,768]{4,2,3,1,0:T(4,128)}, u32[]{:S(2)}) copy-start(f32[1,2,4,12,768]{4,2,3,1,0:T(4,128)} %param.16) | copy-start | bytes 884740
  9.7 59.7 %copy-start.3 = (bf16[1,2,4,12,768]{4,2,3,1,0:T(4,128)(2,1)S(1)}, bf16[1,2,4,12,768]{4,2,3,1,0:T(4,128)(2,1)}, u32[]{:S(2)}) copy-start(bf16[1,2,4,12,768]{4,2,3,1,0:T(4,128)(2,1)} %param.15) | copy-start | bytes 442372
  69.4 35.8 %copy-start = (f32[1,2,2,12,3072]{4,2,3,1,0:T(2,128)S(1)}, f32[1,2,2,12,3072]{4,2,3,1,0:T(2,128)}, u32[]{:S(2)}) copy-start(f32[1,2,2,12,3072]{4,2,3,1,0:T(2,128)} %param.22) | copy-start | bytes 1769476
  69.4 35.8 %copy-start.1 = (bf16[1,2,2,12,3072]{4,2,3,1,0:T(2,128)(2,1)S(1)}, bf16[1,2,2,12,3072]{4,2,3,1,0:T(2,128)(2,1)}, u32[]{:S(2)}) copy-start(bf16[1,2,2,12,3072]{4,2,3,1,0:T(2,128)(2,1)} %param.21) | copy-start | bytes 884740
  71.5 63.5 %copy-start.11 = (f32[2,4,3,32,32]{4,3,2,1,0:T(8,128)S(1)}, f32[2,4,3,32,32]{4,3,2,1,0:T(8,128)}, u32[]{:S(2)}) copy-start(f32[2,4,3,32,32]{4,3,2,1,0:T(8,128)} %param.18) | copy-start | bytes 294916
  111.3 25.7 %copy-start.12 = (f32[2,2,3,32,32]{4,3,2,1,0:T(8,128)S(1)}, f32[2,2,3,32,32]{4,3,2,1,0:T(8,128)}, u32[]{:S(2)}) copy-start(f32[2,2,3,32,32]{4,3,2,1,0:T(8,128)} %param.24) | copy-start | bytes 147460
  140.0 201.3 %copy-start.15 = (bf16[1,2,156]{2,1,0:T(2,128)(2,1)S(1)}, bf16[1,2,156]{2,1,0:T(2,128)(2,1)}, u32[]{:S(2)}) copy-start(bf16[1,2,156]{2,1,0:T(2,128)(2,1)} %param.27) | copy-start | bytes 1876
  140.0 289.3 %all-reduce.17.cloned.1.call-start = ((), (), s32[]{:S(2)}) async-start(), calls=%async_computation.4 | async-start | bytes 4718592 | tf_op jit(solution)/shard_map/psum | solution.py:12
  341.1 332.5 %all-reduce.11.cloned.1.call-start = ((), (), s32[]{:S(2)}) async-start(), calls=%async_computation.1 | async-start | bytes 4718592 | tf_op jit(solution)/shard_map/psum | solution.py:11
  429.3 2.9 copy-start.6
  463.9 211.0 %copy-start.13 = (f32[2,156]{1,0:T(2,128)S(1)}, f32[2,156]{1,0:T(2,128)}, u32[]{:S(2)}) copy-start(f32[2,156]{1,0:T(2,128)} %param.29) | copy-start | bytes 3748
  463.9 211.0 %copy-start.14 = (f32[2,156]{1,0:T(2,128)S(1)}, f32[2,156]{1,0:T(2,128)}, u32[]{:S(2)}) copy-start(f32[2,156]{1,0:T(2,128)} %param.28) | copy-start | bytes 3748
  463.9 297.8 %all-reduce.15.cloned.1.call-start = ((), (), s32[]{:S(2)}) async-start(), calls=%async_computation.3 | async-start | bytes 4718592 | tf_op jit(solution)/shard_map/psum | solution.py:12
  673.5 90.2 %copy-start.9 = (f32[2,4,12,768]{3,1,2,0:T(4,128)S(1)}, f32[2,4,12,768]{3,1,2,0:T(4,128)}, u32[]{:S(2)}) copy-start(f32[2,4,12,768]{3,1,2,0:T(4,128)} %param.20) | copy-start | bytes 884740
  673.6 90.2 %copy-start.10 = (f32[2,4,12,768]{3,1,2,0:T(4,128)S(1)}, f32[2,4,12,768]{3,1,2,0:T(4,128)}, u32[]{:S(2)}) copy-start(f32[2,4,12,768]{3,1,2,0:T(4,128)} %param.19) | copy-start | bytes 884740
  761.7 2.1 copy-start.5
  764.5 2.7 copy-start.4
  767.2 1.1 copy-start.7
  767.2 1.2 copy-start.8
Sparse Core Ops, SparseCore 0:
  11.9 93.1 all-gather.1
  140.1 200.8 all-reduce.12
  343.5 85.8 all-reduce.16
  464.0 209.4 all-reduce.10
  675.8 85.8 all-reduce.14
